TPU v7x, 256 devices: a whole 4x4x8 slice. The times are simulated.
256 devices in a mesh: rep: 8 (over x, core), own: 32 (over y, z).
Axes of the slice: x: 4, y: 4, z: 8, core: 2. Of those that a mesh axis runs over, the one named last changes fastest.
Arguments:
- replica_weights: float32 [8, 64, 512, 512], P('rep', None, 'own'), may hold values from -6 to 6
- global_weights: float32 [64, 512, 512], P(None, 'own'), may hold values from -6 to 6
- momentum: float32 [96, 512, 512], P('own'), may hold values from -4 to 4
- owners: int32 [64], replicated, may hold values from 0 to 31, as said below
Outputs:
- new_weights: float32 [64, 512, 512], P(None, 'own')
- new_momentum: float32 [96, 512, 512], P('own')
Inputs may be any that keep to these rules, and one draw needn't show every extreme that they name: `owners`: no device owns more than 3 tiles, and some device owns exactly 3.
All inputs are finite; a program needn't handle non-finite values.
Results may differ from a plain program's by a relative error of at most 0.00016.
Values sent between devices are 32-bit elements; how exact they have to be, the bound alone decides.
A program may use at most 64 MiB of HBM per device.

v0:
```python
import jax
import jax.numpy as jnp
from jax import lax
from jax.sharding import PartitionSpec as P

outer_rate = 0.7
momentum_decay = 0.5


def selection(owners, own_count, slot_count):
    count = owners.shape[0]
    position = jnp.arange(count, dtype=jnp.int32)
    earlier = (owners[:, None] == owners[None, :]) & (position[None, :] < position[:, None])
    rank = jnp.sum(earlier.astype(jnp.int32), axis=1)
    slot_id = owners * slot_count + rank
    every_slot = jnp.arange(own_count * slot_count, dtype=jnp.int32)
    return (slot_id[None, :] == every_slot[:, None]).astype(jnp.float32)


def shards(replica_weights, global_weights, momentum, owners):
    own_count = lax.axis_size("own")
    rep_count = lax.axis_size("rep")
    slot_count = momentum.shape[0]
    tile_count, row_count, col_count = global_weights.shape
    slot_table = selection(owners, own_count, slot_count)
    own_index = lax.axis_index("own")
    own_slots = lax.dynamic_slice_in_dim(slot_table, own_index * slot_count, slot_count, 0)
    filled = jnp.sum(own_slots, axis=1)[:, None, None]
    difference = global_weights - replica_weights[0]
    piece_count = difference.shape[1]
    outgoing = jnp.dot(
        slot_table,
        difference.reshape(tile_count, piece_count * col_count),
        precision=lax.Precision.HIGHEST,
    )
    outgoing = outgoing.reshape(own_count * slot_count, piece_count, col_count)
    gathered = lax.all_to_all(outgoing, "own", split_axis=0, concat_axis=1, tiled=True)
    outer_grad = lax.psum(gathered, "rep") / rep_count
    new_momentum = (momentum_decay * momentum + outer_grad) * filled
    returned = lax.all_to_all(
        outer_grad + momentum_decay * new_momentum, "own", split_axis=1, concat_axis=0, tiled=True
    )
    piece_count = returned.shape[1]
    picked = jnp.dot(
        slot_table.T,
        returned.reshape(own_count * slot_count, piece_count * col_count),
        precision=lax.Precision.HIGHEST,
    )
    update = picked.reshape(tile_count, piece_count, col_count)
    new_weights = global_weights - outer_rate * update
    return (new_weights, new_momentum)


def solution(mesh):
    return jax.shard_map(
        shards,
        mesh=mesh,
        in_specs=(P("rep", None, "own", None), P(None, "own", None), P("own", None, None), P()),
        out_specs=(P(None, "own", None), P("own", None, None)),
        check_vma=False,
    )
```

profile of v0, /device:TPU:7, one launch (start us, length us, event | category | flops | bytes accessed | tf_op | source)
XLA Modules:
  0.0 300.4 jit_solution(1551482342381695741)
XLA Ops:
  7.2 0.0 all-reduce.2.cloned.1.call-start
  7.2 0.9 convert_reduce_fusion.1
  8.1 0.7 multiply_add_fusion.1
  8.8 2.7 bitcast_subtract_fusion
  11.5 2.8 fusion.3
  14.3 1.8 copy.31
  16.2 80.6 %all_to_all.33 = f32[96,16,512]{2,1,0:T(8,128)S(1)} all-to-all(f32[96,16,512]{2,1,0:T(8,128)S(1)} %copy.31), channel_id=1, replica_groups=mesh['rep'=8,'own'=32] {'own'}, dimensions={0} | all-to-all | bytes 6291456 | tf_op jit(solution)/shard_map/all_to_all | solution.py:37
  96.7 2.0 copy.32
  98.7 0.0 copy-start.1
  98.7 0.0 all-reduce.2.cloned.1.call-update
  98.7 0.1 iota_compare_fusion
  98.8 0.1 convert_reduce_fusion
  98.9 74.3 %all-reduce.2.cloned.1.call-done = f32[3,512,512]{2,1,0:T(8,128)} async-done(((f32[3,512,512]{2,1,0:T(8,128)}), f32[3,512,512]{2,1,0:T(8,128)}) %all-reduce.2.cloned.1.call-update) | async-done | bytes 3145744 | tf_op jit(solution)/shard_map/psum | solution.py:38
  173.2 0.0 copy-done.1
  173.2 4.5 %multiply_add_fusion = (f32[3,512,512]{2,1,0:T(8,128)S(1)}, f32[3,512,512]{2,1,0:T(8,128)}) fusion(f32[3,512,512]{2,1,0:T(8,128)} %all-reduce.2.cloned.1.call-done, f32[3]{0:T(128)S(1)} %convert_reduce_fusion, f32[3,512,512]{2,1,0:T(8,128)S(1)} %copy-done.1), kind=kLoop, calls=%fused_computation.3 | loop fusion | flops 4718592 | bytes 12582924 | tf_op jit(solution)/shard_map/add | solution.py:41
  177.7 2.2 copy.33
  179.8 104.9 %all_to_all.34 = f32[3,512,512]{2,0,1:T(4,128)S(1)} all-to-all(f32[3,512,512]{2,0,1:T(4,128)S(1)} %copy.33), channel_id=1, replica_groups=mesh['rep'=8,'own'=32] {'own'}, dimensions={1} | all-to-all | bytes 6291456 | tf_op jit(solution)/shard_map/all_to_all | solution.py:40
  284.7 0.0 copy-start
  284.7 1.3 copy.34
  286.0 0.3 copy-done
  286.3 4.7 %copy_subtract_fusion = f32[64,16,512]{2,0,1:T(8,128)S(1)} fusion(f32[64,16,512]{2,1,0:T(8,128)S(1)} %copy-done, s32[64]{0:T(128)S(1)} %multiply_add_fusion.1, f32[12,8,16,512]{3,2,1,0:T(8,128)S(1)} %bitcast.40), kind=kOutput, calls=%fused_computation.9 | convolution fusion | flops 605034496 | bytes 7340288 | tf_op jit(solution)/shard_map/dot_general | solution.py:44
  291.0 2.5 copy.37
Async XLA Ops:
  7.2 166.0 %all-reduce.2.cloned.1.call-start = ((), (), s32[]{:S(2)}) async-start(), calls=%async_computation.2 | async-start | bytes 6291456 | tf_op jit(solution)/shard_map/psum | solution.py:38
  98.7 74.5 %copy-start.1 = (f32[3,512,512]{2,1,0:T(8,128)S(1)}, f32[3,512,512]{2,1,0:T(8,128)}, u32[]{:S(2)}) copy-start(f32[3,512,512]{2,1,0:T(8,128)} %param.6) | copy-start | bytes 9437188
  284.7 1.6 copy-start
Sparse Core Ops, SparseCore 0:
  98.9 74.2 all-reduce.1
where the time goes:
time: 301 us; the launch traced here: 300 us
  blocking collectives  185 us (61%)
  waiting for transfers between devices  74.3 us (25%)
  between operations  14.1 us (5%)
  local copies, waits for them, and re-layouts  10.1 us (3%)
  other arithmetic  8.9 us (3%)
  matrix products  7.53 us (3%)
    all_to_all x1, blocking collectives, shards(): lax.all_to_all(outer_grad + momentum_decay * new_momentum, 'own', split_a...  105 us
    all_to_all x1, blocking collectives, shards(): lax.all_to_all(outgoing, 'own', split_axis=0, concat_axis=1, tiled=True)  80.6 us
    psum x1, waiting for transfers between devices, shards(): outer_grad = lax.psum(gathered, 'rep') / rep_count  74.3 us
  transfers between devices with their start and end apart: 1, of which 1 were waited for; matrix products, arithmetic and copies ran while one was open for 0% of the time, Pallas kernels for 0%

commit v1 on v0

--- a/solution.py
+++ b/solution.py
@@ -37,8 +37,16 @@
     gathered = lax.all_to_all(outgoing, "own", split_axis=0, concat_axis=1, tiled=True)
     outer_grad = lax.psum(gathered, "rep") / rep_count
     new_momentum = (momentum_decay * momentum + outer_grad) * filled
-    returned = lax.all_to_all(
-        outer_grad + momentum_decay * new_momentum, "own", split_axis=1, concat_axis=0, tiled=True
+    returned = jnp.concatenate(
+        lax.all_to_all(
+            jnp.stack(
+                jnp.split(outer_grad + momentum_decay * new_momentum, lax.axis_size("own"), axis=1)
+            ),
+            "own",
+            0,
+            0,
+        ),
+        axis=0,
     )
     piece_count = returned.shape[1]
     picked = jnp.dot(

time: 301 us -> 275 us (0.914)
  blocking collectives: 185 us -> 163 us
  local copies, waits for them, and re-layouts: 10.1 us -> 6.64 us
    all_to_all x1, blocking collectives: 105 us -> 82.5 us  [shards(): lax.all_to_all(jnp.stack(jnp.split(outer_grad + momentum_decay * new_mome...]
where the time goes in v1:
time: 275 us
  blocking collectives  163 us (59%)
  waiting for transfers between devices  74.3 us (27%)
  between operations  14.3 us (5%)
  other arithmetic  8.9 us (3%)
  matrix products  7.45 us (3%)
  local copies, waits for them, and re-layouts  6.64 us (2%)
    all_to_all x1, blocking collectives, shards(): lax.all_to_all(jnp.stack(jnp.split(outer_grad + momentum_decay * new_mome...  82.5 us
    all_to_all x1, blocking collectives, shards(): lax.all_to_all(outgoing, 'own', split_axis=0, concat_axis=1, tiled=True)  80.6 us
    psum x1, waiting for transfers between devices, shards(): outer_grad = lax.psum(gathered, 'rep') / rep_count  74.3 us
  transfers between devices with their start and end apart: 1, of which 1 were waited for; matrix products, arithmetic and copies ran while one was open for 0% of the time, Pallas kernels for 0%

profile of v1, /device:TPU:7, one launch (start us, length us, event | category | flops | bytes accessed | tf_op | source)
XLA Modules:
  0.0 274.7 jit_solution(14647033289377143857)
XLA Ops:
  7.2 0.0 all-reduce.2.cloned.1.call-start
  7.2 0.9 convert_reduce_fusion.1
  8.1 0.7 multiply_add_fusion.1
  8.8 2.7 bitcast_subtract_fusion
  11.5 2.8 %fusion.3 = f32[96,16,512]{2,0,1:T(8,128)S(1)} fusion(s32[64]{0:T(128)S(1)} %multiply_add_fusion.1, f32[8,8,16,512]{3,2,1,0:T(8,128)S(1)} %bitcast.167), kind=kOutput, calls=%fused_computation.5 | convolution fusion | flops 603985920 | bytes 5243136 | tf_op jit(solution)/shard_map/dot_general | solution.py:31
  14.3 1.8 copy.27
  16.2 80.6 %all_to_all.23 = f32[96,16,512]{2,1,0:T(8,128)S(1)} all-to-all(f32[96,16,512]{2,1,0:T(8,128)S(1)} %copy.27), channel_id=1, replica_groups=mesh['rep'=8,'own'=32] {'own'}, dimensions={0} | all-to-all | bytes 6291456 | tf_op jit(solution)/shard_map/all_to_all | solution.py:37
  96.7 2.0 copy.28
  98.7 0.0 copy-start.1
  98.7 0.0 all-reduce.2.cloned.1.call-update
  98.7 0.1 iota_compare_fusion
  98.8 0.1 convert_reduce_fusion
  98.9 74.3 %all-reduce.2.cloned.1.call-done = f32[3,512,512]{2,1,0:T(8,128)} async-done(((f32[3,512,512]{2,1,0:T(8,128)}), f32[3,512,512]{2,1,0:T(8,128)}) %all-reduce.2.cloned.1.call-update) | async-done | bytes 3145744 | tf_op jit(solution)/shard_map/psum | solution.py:38
  173.2 0.0 copy-done.1
  173.2 4.5 %multiply_add_fusion = (f32[3,512,512]{2,1,0:T(8,128)S(1)}, f32[3,512,512]{2,1,0:T(8,128)}) fusion(f32[3,512,512]{2,1,0:T(8,128)} %all-reduce.2.cloned.1.call-done, f32[3]{0:T(128)S(1)} %convert_reduce_fusion, f32[3,512,512]{2,1,0:T(8,128)S(1)} %copy-done.1), kind=kLoop, calls=%fused_computation.3 | loop fusion | flops 4718592 | bytes 12582924 | tf_op jit(solution)/shard_map/add | solution.py:43
  178.2 0.0 copy-start
  178.2 82.5 %all_to_all.24 = f32[32,3,16,512]{3,2,1,0:T(8,128)S(1)} all-to-all(f32[32,3,16,512]{3,2,1,0:T(8,128)S(1)} %fusion.8), channel_id=1, replica_groups=mesh['rep'=8,'own'=32] {'own'}, dimensions={0} | all-to-all | bytes 6291456 | tf_op jit(solution)/shard_map/all_to_all | solution.py:41
  260.8 0.0 copy-done
  260.8 4.6 %copy_subtract_fusion = f32[64,16,512]{2,0,1:T(8,128)S(1)} fusion(f32[64,16,512]{2,1,0:T(8,128)S(1)} %copy-done, s32[64]{0:T(128)S(1)} %multiply_add_fusion.1, f32[12,8,16,512]{3,2,1,0:T(8,128)S(1)} %bitcast.166), kind=kOutput, calls=%fused_computation.9 | convolution fusion | flops 605034496 | bytes 7340288 | tf_op jit(solution)/shard_map/dot_general | solution.py:52
  265.4 2.5 copy.31
  (32 shorter events, 0.3 us)
Async XLA Ops:
  7.2 166.0 %all-reduce.2.cloned.1.call-start = ((), (), s32[]{:S(2)}) async-start(), calls=%async_computation.2 | async-start | bytes 6291456 | tf_op jit(solution)/shard_map/psum | solution.py:38
  98.7 74.5 %copy-start.1 = (f32[3,512,512]{2,1,0:T(8,128)S(1)}, f32[3,512,512]{2,1,0:T(8,128)}, u32[]{:S(2)}) copy-start(f32[3,512,512]{2,1,0:T(8,128)} %param.6) | copy-start | bytes 9437188
  178.2 82.6 %copy-start = (f32[64,16,512]{2,1,0:T(8,128)S(1)}, f32[64,16,512]{2,1,0:T(8,128)}, u32[]{:S(2)}) copy-start(f32[64,16,512]{2,1,0:T(8,128)} %param.5) | copy-start | bytes 6291460
Sparse Core Ops, SparseCore 0:
  98.9 74.2 all-reduce.1

commit v2 on v0

--- a/solution.py
+++ b/solution.py
@@ -35,7 +35,7 @@
     )
     outgoing = outgoing.reshape(own_count * slot_count, piece_count, col_count)
     gathered = lax.all_to_all(outgoing, "own", split_axis=0, concat_axis=1, tiled=True)
-    outer_grad = lax.psum(gathered, "rep") / rep_count
+    outer_grad = jnp.sum(lax.all_gather(gathered, "rep"), axis=0) / rep_count
     new_momentum = (momentum_decay * momentum + outer_grad) * filled
     returned = lax.all_to_all(
         outer_grad + momentum_decay * new_momentum, "own", split_axis=1, concat_axis=0, tiled=True

time: 301 us -> 361 us (1.20); the launches traced: 300 us -> 356 us
  waiting for transfers between devices: 74.3 us -> 123 us
  other arithmetic: 8.9 us -> 19 us
    all_gather x0 -> x1, waiting for transfers between devices: none -> 123 us  [shards(): outer_grad = jnp.sum(lax.all_gather(gathered, 'rep'), axis=0) / rep_count]
    psum x1 -> x0, waiting for transfers between devices: 74.3 us -> none  [shards(): outer_grad = lax.psum(gathered, 'rep') / rep_count]
    reduce_sum x0 -> x1, other arithmetic: none -> 10.1 us  [shards(): outer_grad = jnp.sum(lax.all_gather(gathered, 'rep'), axis=0) / rep_count]
where the time goes in v2:
time: 361 us; the launch traced here: 356 us
  blocking collectives  183 us (51%)
  waiting for transfers between devices  123 us (34%)
  other arithmetic  19 us (5%)
  between operations  14.1 us (4%)
  local copies, waits for them, and re-layouts  10.1 us (3%)
  matrix products  7.52 us (2%)
    all_gather x1, waiting for transfers between devices, shards(): outer_grad = jnp.sum(lax.all_gather(gathered, 'rep'), axis=0) / rep_count  123 us
    all_to_all x1, blocking collectives, shards(): lax.all_to_all(outer_grad + momentum_decay * new_momentum, 'own', split_a...  102 us
    all_to_all x1, blocking collectives, shards(): lax.all_to_all(outgoing, 'own', split_axis=0, concat_axis=1, tiled=True)  80.6 us
    reduce_sum x1, other arithmetic, shards(): outer_grad = jnp.sum(lax.all_gather(gathered, 'rep'), axis=0) / rep_count  10.1 us
  transfers between devices with their start and end apart: 1, of which 1 were waited for; matrix products, arithmetic and copies ran while one was open for 0% of the time, Pallas kernels for 0%

profile of v2, /device:TPU:7, one launch (start us, length us, event | category | flops | bytes accessed | tf_op | source)
XLA Modules:
  0.0 356.3 jit_solution(2015816193430337802)
XLA Ops:
  7.2 0.0 all-gather.2.cloned.1.call-start
  7.2 0.9 convert_reduce_fusion.1
  8.1 0.7 multiply_add_fusion.1
  8.8 2.7 bitcast_subtract_fusion
  11.5 2.8 fusion.3
  14.3 1.8 copy.33
  16.2 80.6 %all_to_all.30 = f32[96,16,512]{2,1,0:T(8,128)S(1)} all-to-all(f32[96,16,512]{2,1,0:T(8,128)S(1)} %copy.33), channel_id=1, replica_groups=mesh['rep'=8,'own'=32] {'own'}, dimensions={0} | all-to-all | bytes 6291456 | tf_op jit(solution)/shard_map/all_to_all | solution.py:37
  96.7 2.0 copy.34
  98.7 0.0 all-gather.2.cloned.1.call-update
  98.7 0.1 iota_compare_fusion
  98.8 0.1 convert_reduce_fusion
  98.9 122.8 %all-gather.2.cloned.1.call-done = f32[8,3,512,512]{3,2,1,0:T(8,128)} async-done(((f32[1,3,512,512]{3,2,1,0:T(8,128)}), f32[8,3,512,512]{3,2,1,0:T(8,128)}) %all-gather.2.cloned.1.call-update) | async-done | bytes 25165840 | tf_op jit(solution)/shard_map/all_gather | solution.py:38
  221.7 10.1 %reduce_sum.28 = f32[3,512,512]{2,1,0:T(8,128)S(1)} reduce(f32[8,3,512,512]{3,2,1,0:T(8,128)} %all-gather.2.cloned.1.call-done, f32[]{:T(128)} %constant.2.clone.1), dimensions={0}, to_apply=%region_1.0 | reduce | flops 5505024 | bytes 28311556 | tf_op jit(solution)/shard_map/reduce_sum | solution.py:38
  231.8 4.5 %multiply_add_fusion = (f32[3,512,512]{2,1,0:T(8,128)S(1)}, f32[3,512,512]{2,1,0:T(8,128)}) fusion(f32[3,512,512]{2,1,0:T(8,128)S(1)} %reduce_sum.28, f32[3]{0:T(128)S(1)} %convert_reduce_fusion, f32[3,512,512]{2,1,0:T(8,128)} %param.6), kind=kLoop, calls=%fused_computation.3 | loop fusion | flops 4718592 | bytes 12582924 | tf_op jit(solution)/shard_map/add | solution.py:41
  236.3 2.2 copy.35
  238.4 102.2 %all_to_all.31 = f32[3,512,512]{2,0,1:T(4,128)S(1)} all-to-all(f32[3,512,512]{2,0,1:T(4,128)S(1)} %copy.35), channel_id=1, replica_groups=mesh['rep'=8,'own'=32] {'own'}, dimensions={1} | all-to-all | bytes 6291456 | tf_op jit(solution)/shard_map/all_to_all | solution.py:40
  340.6 0.0 copy-start
  340.6 1.3 copy.36
  342.0 0.3 copy-done
  342.2 4.7 %copy_subtract_fusion = f32[64,16,512]{2,0,1:T(8,128)S(1)} fusion(f32[64,16,512]{2,1,0:T(8,128)S(1)} %copy-done, s32[64]{0:T(128)S(1)} %multiply_add_fusion.1, f32[12,8,16,512]{3,2,1,0:T(8,128)S(1)} %bitcast.40), kind=kOutput, calls=%fused_computation.9 | convolution fusion | flops 605034496 | bytes 7340288 | tf_op jit(solution)/shard_map/dot_general | solution.py:44
  346.9 2.5 copy.39
Async XLA Ops:
  7.2 214.6 %all-gather.2.cloned.1.call-start = ((), (), s32[]{:S(2)}) async-start(), calls=%async_computation.2 | async-start | bytes 28311552 | tf_op jit(solution)/shard_map/all_gather | solution.py:38
  340.6 1.6 copy-start
Sparse Core Ops, SparseCore 0:
  98.9 122.8 all-gather.1
